TPU v7x, 32 devices: a whole 2x2x4 slice. The times are simulated.
32 devices in a mesh: pb: 8 (over y, x, core), ka: 4 (over z).
Axes of the slice: x: 2, y: 2, z: 4, core: 2. Of those that a mesh axis runs over, the one named last changes fastest.
Arguments:
- coupling: bfloat16 [2, 320, 4800, 320], P(None, 'ka', 'pb'), may hold values from -0.019897461 to 0.019897461
- kpoints: int32 [3, 16], replicated, may hold values from 0 to 99
- qpoints: int32 [3, 32], replicated, may hold values from 0 to 99
- electron_cells: int32 [3, 320], replicated, may hold values from -6 to 6
- phonon_cells: int32 [3, 320], replicated, may hold values from -6 to 6
- phonon_modes: bfloat16 [32, 2, 120, 120], P('pb'), may hold values from -0.375 to 0.375
- band_vectors: bfloat16 [32, 16, 2, 40, 40], P('pb', 'ka'), may hold values from -0.625 to 0.625
- energies_kq: float32 [32, 16, 40], P('pb', 'ka'), may hold values from -0.5 to 0.5
- occupations_kq: float32 [32, 16, 40], P('pb', 'ka'), may hold values from 0 to 1
- energy_k: float32 [16], P('ka'), may hold values from -0.5 to 0.5
- occupation_k: float32 [16], P('ka'), may hold values from 0 to 1
- frequencies: float32 [32, 120], P('pb'), may hold values from 0.02 to 0.2
- bose_factors: float32 [32, 120], P('pb'), may hold values from 0.1 to 5
Outputs:
- electron_width: float32 [16, 120], P('ka')
- phonon_width: float32 [32, 120], P('pb')
All inputs are finite; a program needn't handle non-finite values.
Results may differ from a plain program's by a relative error of at most 0.0066.
Values may be sent and summed in bfloat16 or wider, within the bound.
A program may use at most 320 MiB of HBM per device.

v0:
```python
import math

import jax
import jax.numpy as jnp
from jax import lax
from jax.sharding import PartitionSpec as P

NB = 40
MODES = 120
NG = 100


smearing = 0.05


def phase_table(points, cells):
    product = (
        points[0][:, None] * cells[0][None, :]
        + points[1][:, None] * cells[1][None, :]
        + points[2][:, None] * cells[2][None, :]
    )
    angle = jnp.mod(product, NG).astype(jnp.float32) * (2.0 * math.pi / NG)
    return (jnp.cos(angle).astype(jnp.bfloat16), jnp.sin(angle).astype(jnp.bfloat16))


def gaussian(offset):
    return jnp.exp(-0.5 * (offset / smearing) ** 2) / (smearing * math.sqrt(2.0 * math.pi))


def contract_last(left, right):
    return lax.dot_general(
        left, right, (((1,), (1,)), ((), ())), preferred_element_type=jnp.float32
    )


def mixed(form, left, right):
    return jnp.einsum(form, left, right, preferred_element_type=jnp.float32)


def widths(
    bloch_real, bloch_imag, modes, vectors, levels, filled, energy_k, occupation_k, omega, bose
):
    mode_real = modes[:, 0]
    mode_imag = modes[:, 1]
    moded_real = (
        mixed("kqnm,qmv->kqnv", bloch_real, mode_real)
        - mixed("kqnm,qmv->kqnv", bloch_imag, mode_imag)
    ).astype(jnp.bfloat16)
    moded_imag = (
        mixed("kqnm,qmv->kqnv", bloch_real, mode_imag)
        + mixed("kqnm,qmv->kqnv", bloch_imag, mode_real)
    ).astype(jnp.bfloat16)
    vector_real = vectors[:, :, 0]
    vector_imag = vectors[:, :, 1]
    band_real = mixed("qknb,kqnv->kqbv", vector_real, moded_real) + mixed(
        "qknb,kqnv->kqbv", vector_imag, moded_imag
    )
    band_imag = mixed("qknb,kqnv->kqbv", vector_real, moded_imag) - mixed(
        "qknb,kqnv->kqbv", vector_imag, moded_real
    )
    weight = band_real * band_real + band_imag * band_imag
    level_kq = jnp.transpose(levels, (1, 0, 2))[..., None]
    filled_kq = jnp.transpose(filled, (1, 0, 2))[..., None]
    offset = energy_k[:, None, None, None] - level_kq
    freq = omega[None, :, None, :]
    boson = bose[None, :, None, :]
    absorb = gaussian(offset + freq)
    emit = gaussian(offset - freq)
    electron = jnp.sum(
        weight * ((boson + filled_kq) * absorb + (boson + 1.0 - filled_kq) * emit), axis=(1, 2)
    )
    phonon = jnp.sum(weight * (occupation_k[:, None, None, None] - filled_kq) * absorb, axis=(0, 2))
    return (electron, phonon)


def on_device(
    coupling,
    kpoints,
    qpoints,
    electron_cells,
    phonon_cells,
    phonon_modes,
    band_vectors,
    energies_kq,
    occupations_kq,
    energy_k,
    occupation_k,
    frequencies,
    bose_factors,
):
    k_local = energy_k.shape[0]
    q_local = frequencies.shape[0]
    cells_local = coupling.shape[1]
    pairs_local = coupling.shape[2]
    phonon_count = coupling.shape[3]
    q_total = q_local * lax.axis_size("pb")
    k_total = k_local * lax.axis_size("ka")
    cos_q, sin_q = phase_table(qpoints, phonon_cells)
    cos_k, sin_k = phase_table(kpoints, electron_cells)
    real_flat = coupling[0].reshape(cells_local * pairs_local, phonon_count)
    imag_flat = coupling[1].reshape(cells_local * pairs_local, phonon_count)
    half_real = (
        (contract_last(cos_q, real_flat) - contract_last(sin_q, imag_flat))
        .astype(jnp.bfloat16)
        .reshape(q_total, cells_local, pairs_local)
    )
    half_imag = (
        (contract_last(cos_q, imag_flat) + contract_last(sin_q, real_flat))
        .astype(jnp.bfloat16)
        .reshape(q_total, cells_local, pairs_local)
    )
    cell_start = lax.axis_index("ka") * cells_local
    cos_cols = lax.dynamic_slice_in_dim(cos_k, cell_start, cells_local, 1)
    sin_cols = lax.dynamic_slice_in_dim(sin_k, cell_start, cells_local, 1)
    real_part = mixed("kr,qrp->kqp", cos_cols, half_real) - mixed(
        "kr,qrp->kqp", sin_cols, half_imag
    )
    imag_part = mixed("kr,qrp->kqp", cos_cols, half_imag) + mixed(
        "kr,qrp->kqp", sin_cols, half_real
    )
    partials = lax.psum_scatter(
        jnp.stack([real_part, imag_part], axis=1), "ka", scatter_dimension=0, tiled=True
    )
    owned_real = partials[:, 0].astype(jnp.bfloat16)
    owned_imag = partials[:, 1].astype(jnp.bfloat16)
    bloch_real, bloch_imag = (
        lax.all_to_all(owned_real, "pb", split_axis=1, concat_axis=2, tiled=True),
        lax.all_to_all(owned_imag, "pb", split_axis=1, concat_axis=2, tiled=True),
    )
    bloch_real = bloch_real.reshape(k_local, q_local, NB, MODES)
    bloch_imag = bloch_imag.reshape(k_local, q_local, NB, MODES)
    electron, phonon = widths(
        bloch_real,
        bloch_imag,
        phonon_modes,
        band_vectors,
        energies_kq,
        occupations_kq,
        energy_k,
        occupation_k,
        frequencies,
        bose_factors,
    )
    electron_width = lax.psum(electron / (q_total * NB), "pb")
    phonon_width = lax.psum(phonon / (k_total * NB), "ka")
    return (electron_width, phonon_width)


def solution(mesh):
    in_specs = (
        P(None, "ka", "pb", None),
        P(),
        P(),
        P(),
        P(),
        P("pb", None, None, None),
        P("pb", "ka", None, None, None),
        P("pb", "ka", None),
        P("pb", "ka", None),
        P("ka"),
        P("ka"),
        P("pb", None),
        P("pb", None),
    )
    out_specs = (P("ka", None), P("pb", None))
    return jax.shard_map(
        on_device, mesh=mesh, in_specs=in_specs, out_specs=out_specs, check_vma=False
    )
```

profile of v0, /device:TPU:0, one launch (start us, length us, event | category | flops | bytes accessed | tf_op | source)
XLA Modules:
  0.0 401.3 jit_solution(5128151231587418274)
XLA Ops:
  7.2 0.0 reduce-scatter.2.cloned.1.call-start
  7.2 0.8 slice_reduce_fusion.2
  8.0 0.8 slice_bitcast_fusion.4
  8.8 42.7 %fusion.68 = (bf16[1,80,600,320]{2,3,1,0:T(8,128)(2,1)}, bf16[1,80,600,320]{2,3,1,0:T(8,128)(2,1)}) fusion(bf16[2,80,600,320]{2,3,1,0:T(8,128)(2,1)} %param.13), kind=kLoop, calls=%fused_computation.105 | loop fusion | bytes 122880000 | tf_op jit(solution)/shard_map/slice | solution.py:100
  51.5 34.4 %copy.59 = bf16[1,80,600,320]{2,1,3,0:T(8,128)(2,1)} copy(bf16[1,80,600,320]{2,3,1,0:T(8,128)(2,1)} %get-tuple-element.10) | data formatting | bytes 61440000 | tf_op jit(solution)/shard_map/slice | solution.py:100
  86.0 46.7 %reshape_squeeze.6 = bf16[48000,320]{0,1:T(8,128)(2,1)} reshape(bf16[1,80,600,320]{2,1,3,0:T(8,128)(2,1)} %copy.59) | data formatting | bytes 61440000 | tf_op jit(solution)/shard_map/reshape;squeeze | solution.py:100
  132.7 34.4 %copy.60 = bf16[1,80,600,320]{2,1,3,0:T(8,128)(2,1)} copy(bf16[1,80,600,320]{2,3,1,0:T(8,128)(2,1)} %get-tuple-element.11) | data formatting | bytes 61440000 | tf_op jit(solution)/shard_map/slice | solution.py:101
  167.1 46.7 %reshape_squeeze.7 = bf16[48000,320]{0,1:T(8,128)(2,1)} reshape(bf16[1,80,600,320]{2,1,3,0:T(8,128)(2,1)} %copy.60) | data formatting | bytes 61440000 | tf_op jit(solution)/shard_map/reshape;squeeze | solution.py:101
  213.7 12.6 %fusion.43 = f32[32,48000]{1,0:T(8,128)S(1)} fusion(bf16[48000,320]{0,1:T(8,128)(2,1)} %reshape_squeeze.6, s32[320]{0:T(512)S(1)} %get-tuple-element.8, s32[32]{0:T(128)S(1)} %get-tuple-element.20, s32[320]{0:T(512)S(1)} %get-tuple-element.9, s32[32]{0:T(128)S(1)} %get-tuple-element.21, s32[320]{0:T(512)S(1)} %get-tuple-element.7, s32[32]{0:T(128)S(1)} %get-tuple-element.19), kind=kOutput, calls=%fused_computation.65 | convolution fusion | flops 983183360 | bytes 36868224 | tf_op jit(solution)/shard_map/dot_general | solution.py:31
  226.4 15.4 %fusion.42 = f32[32,48000]{1,0:T(8,128)} fusion(bf16[48000,320]{0,1:T(8,128)(2,1)} %reshape_squeeze.7, s32[320]{0:T(512)S(1)} %get-tuple-element.8, s32[32]{0:T(128)S(1)} %get-tuple-element.20, s32[320]{0:T(512)S(1)} %get-tuple-element.9, s32[32]{0:T(128)S(1)} %get-tuple-element.21, s32[320]{0:T(512)S(1)} %get-tuple-element.7, s32[32]{0:T(128)S(1)} %get-tuple-element.19), kind=kOutput, calls=%fused_computation.64 | convolution fusion | flops 983183360 | bytes 36868224 | tf_op jit(solution)/shard_map/dot_general | solution.py:31
  241.8 14.4 %fusion = bf16[32,48000]{1,0:T(8,128)(2,1)} fusion(f32[32,48000]{1,0:T(8,128)S(1)} %fusion.43, bf16[48000,320]{0,1:T(8,128)(2,1)} %reshape_squeeze.7, s32[320]{0:T(512)S(1)} %get-tuple-element.8, s32[32]{0:T(128)S(1)} %get-tuple-element.20, s32[320]{0:T(512)S(1)} %get-tuple-element.9, s32[32]{0:T(128)S(1)} %get-tuple-element.21, ...), kind=kOutput, calls=%fused_computation.2 | convolution fusion | flops 986255360 | bytes 39940224 | tf_op jit(solution)/shard_map/dot_general | solution.py:31
  256.2 0.0 copy-start.5
  256.2 0.0 copy-start.7
  256.2 6.9 %reshape.41 = bf16[32,80,600]{2,1,0:T(8,128)(2,1)S(1)} reshape(bf16[32,48000]{1,0:T(8,128)(2,1)} %fusion) | data formatting | bytes 6144000 | tf_op jit(solution)/shard_map/reshape | solution.py:105
  263.1 0.0 copy-done.5
  263.2 0.0 copy-done.7
  263.2 16.1 %fusion.1 = bf16[32,48000]{1,0:T(8,128)(2,1)} fusion(f32[32,48000]{1,0:T(8,128)} %fusion.42, bf16[48000,320]{0,1:T(8,128)(2,1)} %reshape_squeeze.6, s32[320]{0:T(512)S(1)} %get-tuple-element.8, s32[32]{0:T(128)S(1)} %get-tuple-element.20, s32[320]{0:T(512)S(1)} %get-tuple-element.9, s32[32]{0:T(128)S(1)} %get-tuple-element.21, s32[320]{0:T(512)S(1)} %get-tuple-element.7, ...), kind=kOutput, calls=%fused_computation.3 | convolution fusion | flops 986255360 | bytes 39940224 | tf_op jit(solution)/shard_map/dot_general | solution.py:31
  279.3 7.8 %reshape.42 = bf16[32,80,600]{2,1,0:T(8,128)(2,1)} reshape(bf16[32,48000]{1,0:T(8,128)(2,1)} %fusion.1) | data formatting | bytes 6144000 | tf_op jit(solution)/shard_map/reshape | solution.py:110
  287.1 0.0 copy-start
  287.1 0.1 fusion.38
  287.2 0.7 fusion.50
  287.8 1.2 copy-done
  289.0 0.7 fusion.48
  289.6 0.7 fusion.3
  290.3 0.7 fusion.2
  291.0 0.2 pad_maximum_fusion
  291.2 0.0 copy-start.2
  291.2 2.3 copy.61
  293.5 0.0 copy-start.6
  293.5 0.0 copy-start.1
  293.5 0.0 reduce-scatter.2.cloned.1.call-update
  293.6 0.0 copy-done.2
  293.6 0.1 copy.81
  293.8 0.1 copy.82
  293.9 0.3 copy-done.4
  294.2 0.0 copy-done.8
  294.2 0.1 subtract_bitcast_fusion
  294.3 0.0 copy-done.3
  294.3 0.0 copy-done.9
  294.3 0.1 broadcast_subtract_fusion
  294.4 54.3 %reduce-scatter.2.cloned.1.call-done = f32[4,2,32,600]{3,2,1,0:T(8,128)} async-done(((f32[16,2,32,600]{3,2,1,0:T(8,128)}), f32[4,2,32,600]{3,2,1,0:T(8,128)}) %reduce-scatter.2.cloned.1.call-update) | async-done | bytes 614416 | tf_op jit(solution)/shard_map/reduce_scatter | solution.py:121
  348.7 1.1 convert.4
  349.9 0.7 copy.62
  350.6 3.6 all-to-all-start
  354.3 0.0 copy-done.6
  354.3 0.7 copy.65
  355.0 5.1 %all-to-all-done = bf16[4,32,600]{2,0,1:T(4,128)(2,1)S(1)} async-done(((bf16[4,32,600]{2,0,1:T(4,128)(2,1)}), bf16[4,32,600]{2,0,1:T(4,128)(2,1)S(1)}, u32[]{:S(2)}, u32[]{:S(2)}) %all-to-all-start) | async-done | bytes 153632 | tf_op jit(solution)/shard_map/all_to_all | solution.py:127
  360.1 3.6 all-to-all-start.1
  363.7 0.0 copy-start.10
  363.8 0.3 reshape.43
  364.1 0.0 copy-done.1
  364.1 0.2 fusion.22
  364.3 0.2 fusion.26
  364.6 4.7 %all-to-all-done.1 = bf16[4,32,600]{2,0,1:T(4,128)(2,1)S(1)} async-done(((bf16[4,32,600]{2,0,1:T(4,128)(2,1)}), bf16[4,32,600]{2,0,1:T(4,128)(2,1)S(1)}, u32[]{:S(2)}, u32[]{:S(2)}) %all-to-all-start.1) | async-done | bytes 153632 | tf_op jit(solution)/shard_map/all_to_all | solution.py:128
  369.3 0.3 reshape.44
  369.6 0.2 fusion.10
  369.9 0.2 fusion.11
  370.1 0.2 fusion.14
  370.4 0.2 fusion.16
  370.6 0.2 fusion.7
  370.8 0.0 copy-done.10
  370.8 0.5 multiply_reduce_fusion
  371.3 12.4 %psum.14 = f32[4,120]{1,0:T(4,128)} all-reduce(f32[4,120]{1,0:T(4,128)S(1)} %broadcast_multiply_fusion.1), channel_id=1, replica_groups=mesh['pb'=8,'ka'=4] {'pb'}, use_global_device_ids=true, to_apply=%region_2.3 | all-reduce | flops 480 | bytes 3840 | tf_op jit(solution)/shard_map/psum | solution.py:144
  383.7 10.8 %psum.15 = f32[4,120]{1,0:T(4,128)} all-reduce(f32[4,120]{1,0:T(4,128)S(1)} %broadcast_multiply_fusion), channel_id=1, replica_groups=mesh['pb'=8,'ka'=4] {'ka'}, use_global_device_ids=true, to_apply=%region_4.5 | all-reduce | flops 480 | bytes 3840 | tf_op jit(solution)/shard_map/psum | solution.py:145
  (16 shorter events, 0.2 us)
Async XLA Ops:
  7.2 341.6 %reduce-scatter.2.cloned.1.call-start = ((), (), s32[]{:S(2)}) async-start(), calls=%async_computation.3 | async-start | bytes 3276800 | tf_op jit(solution)/shard_map/reduce_scatter | solution.py:121
  256.2 6.9 %copy-start.5 = (s32[3,320]{1,0:T(4,128)S(1)}, s32[3,320]{1,0:T(4,128)}, u32[]{:S(2)}) copy-start(s32[3,320]{1,0:T(4,128)} %param.16) | copy-start | bytes 11524
  256.2 7.0 %copy-start.7 = (s32[3,16]{1,0:T(4,128)S(1)}, s32[3,16]{1,0:T(4,128)}, u32[]{:S(2)}) copy-start(s32[3,16]{1,0:T(4,128)} %param.14) | copy-start | bytes 580
  287.1 1.9 copy-start
  291.2 2.4 copy-start.2
  293.5 0.7 copy-start.4
  293.5 0.7 copy-start.8
  293.5 0.8 copy-start.3
  293.5 0.8 copy-start.9
  293.5 60.7 %copy-start.6 = (f32[4,120]{1,0:T(4,128)S(1)}, f32[4,120]{1,0:T(4,128)}, u32[]{:S(2)}) copy-start(f32[4,120]{1,0:T(4,128)} %param.25) | copy-start | bytes 5764
  293.5 70.6 %copy-start.1 = (bf16[4,2,120,120]{3,2,1,0:T(8,128)(2,1)S(1)}, bf16[4,2,120,120]{3,2,1,0:T(8,128)(2,1)}, u32[]{:S(2)}) copy-start(bf16[4,2,120,120]{3,2,1,0:T(8,128)(2,1)} %param.18) | copy-start | bytes 691204
  350.6 9.5 %all-to-all-start = ((bf16[4,32,600]{2,0,1:T(4,128)(2,1)}), bf16[4,32,600]{2,0,1:T(4,128)(2,1)S(1)}, u32[]{:S(2)}, u32[]{:S(2)}) async-start(bf16[4,32,600]{2,0,1:T(4,128)(2,1)} %copy.62), calls=%async_computation.1 | async-start | bytes 327680 | tf_op jit(solution)/shard_map/all_to_all | solution.py:127
  360.1 9.2 %all-to-all-start.1 = ((bf16[4,32,600]{2,0,1:T(4,128)(2,1)}), bf16[4,32,600]{2,0,1:T(4,128)(2,1)S(1)}, u32[]{:S(2)}, u32[]{:S(2)}) async-start(bf16[4,32,600]{2,0,1:T(4,128)(2,1)} %copy.65), calls=%async_computation.2 | async-start | bytes 327680 | tf_op jit(solution)/shard_map/all_to_all | solution.py:128
  363.7 7.1 %copy-start.10 = (f32[4,120]{1,0:T(4,128)S(1)}, f32[4,120]{1,0:T(4,128)}, u32[]{:S(2)}) copy-start(f32[4,120]{1,0:T(4,128)} %param.24) | copy-start | bytes 5764
Sparse Core Ops, SparseCore 0:
  293.7 54.9 reduce-scatter.1
where the time goes:
time: 404 us; the launch traced here: 401 us
  local copies, waits for them, and re-layouts  228 us (56%)
  waiting for transfers between devices  64.2 us (16%)
  matrix products  63.3 us (16%)
  blocking collectives  23.1 us (6%)
  between operations  14.3 us (4%)
  starting transfers between devices  7.27 us (2%)
    slice x2, local copies, waits for them, and re-layouts, on_device(): real_flat = coupling[0].reshape(cells_local * pairs_local, phonon_count)  77.2 us
    dot_general x4, matrix products, contract_last(): lax.dot_general(left, right, (((1,), (1,)), ((), ())), preferred_element_...  58.6 us
    reduce_scatter x1, waiting for transfers between devices, on_device(): lax.psum_scatter(jnp.stack([real_part, imag_part], axis=1), 'ka', scatter...  54.3 us
    another operation x1, local copies, waits for them, and re-layouts, on_device(): real_flat = coupling[0].reshape(cells_local * pairs_local, phonon_count)  46.7 us
    another operation x1, local copies, waits for them, and re-layouts, on_device(): imag_flat = coupling[1].reshape(cells_local * pairs_local, phonon_count)  46.7 us
    slice x1, local copies, waits for them, and re-layouts, on_device(): imag_flat = coupling[1].reshape(cells_local * pairs_local, phonon_count)  34.4 us
    psum x1, blocking collectives, on_device(): electron_width = lax.psum(electron / (q_total * NB), 'pb')  12.4 us
    psum x1, blocking collectives, on_device(): phonon_width = lax.psum(phonon / (k_total * NB), 'ka')  10.8 us
  transfers between devices with their start and end apart: 3, of which 3 were waited for; matrix products, arithmetic and copies ran while one was open for 0% of the time, Pallas kernels for 0%

commit v1 on v0

--- a/solution.py
+++ b/solution.py
@@ -1,8 +1,11 @@
+import functools
 import math
 
 import jax
 import jax.numpy as jnp
 from jax import lax
+from jax.experimental import pallas as pl
+from jax.experimental.pallas import tpu as pltpu
 from jax.sharding import PartitionSpec as P
 
 NB = 40
@@ -71,6 +74,228 @@
     )
     phonon = jnp.sum(weight * (occupation_k[:, None, None, None] - filled_kq) * absorb, axis=(0, 2))
     return (electron, phonon)
+
+
+MESH = pl.DeviceIdType.MESH
+LANES = 128
+
+
+def bloch_kernel(
+    cells_block, tile, last, wq_ref, wk_ref, x_ref, out_ref,
+    half, parts, recv, send_sem, recv_sem,
+):
+    pairs_step = pl.program_id(0)
+    cell_step = pl.program_id(1)
+    tiles = pl.num_programs(0)
+    cell_steps = pl.num_programs(1)
+    bands, kas = lax.axis_size("pb"), lax.axis_size("ka")
+    devices = bands * kas
+    me = lax.axis_index("pb") * kas + lax.axis_index("ka")
+    columns = wq_ref.shape[0]
+    cells = half.shape[1] // columns
+    groups = parts.shape[2]
+    mine = groups // bands
+    rows = parts.shape[3] // 2
+    barrier = pltpu.get_barrier_semaphore()
+
+    @pl.when((pairs_step == 0) & (cell_step == 0))
+    def _():
+        def greet(step, carry):
+            peer = lax.rem(me + step, devices)
+            pl.semaphore_signal(
+                barrier, inc=1, device_id={"pb": peer // kas, "ka": lax.rem(peer, kas)},
+                device_id_type=MESH,
+            )
+            return carry
+
+        lax.fori_loop(1, devices, greet, 0)
+
+    for cell in range(cells_block):
+        right = jnp.concatenate([x_ref[0, cell], x_ref[1, cell]], axis=0)
+        product = jnp.dot(wq_ref[...], right, preferred_element_type=jnp.float32)
+        row = cell_step * cells_block + cell
+        for lane in range(tile // LANES):
+            half[lane, pl.ds(row, columns, stride=cells), :] = product[
+                :, lane * LANES : (lane + 1) * LANES
+            ]
+
+    def strip(index):
+        start = pl.multiple_of(index * cells, cells)
+        return jnp.concatenate(
+            [half[lane, pl.ds(start, cells), :] for lane in range(tile // LANES)], axis=1
+        ).astype(jnp.bfloat16)
+
+    @pl.when(cell_step == cell_steps - 1)
+    def _():
+        def contract(group, carry):
+            sums = []
+            for member in range(2):
+                q = group * 2 + member
+                right = jnp.concatenate([strip(q), strip(columns // 2 + q)], axis=0)
+                sums.append(
+                    jnp.dot(wk_ref[...], right, preferred_element_type=jnp.float32)
+                )
+            for ka in range(kas):
+                block = slice(ka * rows, (ka + 1) * rows)
+                parts[pairs_step, ka, group] = jnp.concatenate(
+                    [sums[0][block], sums[1][block]], axis=0
+                ).astype(jnp.bfloat16)
+            return carry
+
+        lax.fori_loop(0, groups, contract, 0, unroll=4)
+
+    @pl.when((cell_step == cell_steps - 1) & (pairs_step == 0))
+    def _():
+        pl.semaphore_wait(barrier, devices - 1)
+
+    def send(index, width):
+        def one(step, carry):
+            peer = lax.rem(me + step, devices)
+            to_pb, to_ka = peer // kas, lax.rem(peer, kas)
+            pltpu.make_async_remote_copy(
+                src_ref=parts.at[index, to_ka, pl.ds(to_pb * mine, mine), :, pl.ds(0, width)],
+                dst_ref=recv.at[index, me, :, :, pl.ds(0, width)],
+                send_sem=send_sem.at[index],
+                recv_sem=recv_sem.at[index],
+                device_id={"pb": to_pb, "ka": to_ka},
+                device_id_type=MESH,
+            ).start()
+            return carry
+
+        lax.fori_loop(1, devices, one, 0)
+
+    @pl.when((cell_step == cell_steps - 1) & (pairs_step < tiles - 1))
+    def _():
+        send(pairs_step, tile)
+
+    @pl.when((cell_step == cell_steps - 1) & (pairs_step == tiles - 1))
+    def _():
+        count = recv.shape[0]
+        send(count - 1, last)
+        my_pb, my_ka = lax.axis_index("pb"), lax.axis_index("ka")
+        for index in range(count):
+            recv[index, me] = parts[index, my_ka, pl.ds(my_pb * mine, mine)]
+        for index in range(count):
+            width = tile if index < count - 1 else last
+            window = recv.at[index, pl.ds(1, devices - 1), :, :, pl.ds(0, width)]
+            pltpu.make_async_copy(window, window, send_sem.at[index]).wait()
+            pltpu.make_async_copy(window, window, recv_sem.at[index]).wait()
+            for band in range(bands):
+                total = recv[index, band * kas, :, :, :width].astype(jnp.float32)
+                for ka in range(1, kas):
+                    total = total + recv[index, band * kas + ka, :, :, :width].astype(jnp.float32)
+                out_ref[band, :, :, index * tile : index * tile + width] = total.astype(
+                    jnp.bfloat16
+                )
+
+
+def bloch(coupling, wq, wk, q_local, k_local):
+    bands, kas = lax.axis_size("pb"), lax.axis_size("ka")
+    devices = bands * kas
+    parts_count, cells, pairs, phonons = coupling.shape
+    moved = jnp.transpose(coupling, (0, 1, 3, 2))
+    padded = -(-pairs // LANES) * LANES
+    if pairs < LANES:
+        moved = jnp.pad(moved, ((0, 0), (0, 0), (0, 0), (0, LANES - pairs)))
+    tile = min(2 * LANES, padded)
+    tiles = -(-padded // tile)
+    last = padded - (tiles - 1) * tile
+    cells_block = 16
+    columns = wq.shape[0]
+    groups = columns // 4
+    mine = q_local // 2
+    rows = 4 * k_local
+    result = pl.pallas_call(
+        functools.partial(bloch_kernel, cells_block, tile, last),
+        grid=(tiles, cells // cells_block),
+        in_specs=[
+            pl.BlockSpec(wq.shape, lambda t, e: (0, 0)),
+            pl.BlockSpec(wk.shape, lambda t, e: (0, 0)),
+            pl.BlockSpec((parts_count, cells_block, phonons, tile), lambda t, e: (0, e, 0, t)),
+        ],
+        out_specs=pl.BlockSpec((bands, mine, rows, padded), lambda t, e: (0, 0, 0, 0)),
+        out_shape=jax.ShapeDtypeStruct((bands, mine, rows, padded), jnp.bfloat16),
+        scratch_shapes=[
+            pltpu.VMEM((tile // LANES, columns * cells, LANES), jnp.float32),
+            pltpu.VMEM((tiles, kas, groups, rows, tile), jnp.bfloat16),
+            pltpu.VMEM((tiles, devices, mine, rows, tile), jnp.bfloat16),
+            pltpu.SemaphoreType.DMA((tiles,)),
+            pltpu.SemaphoreType.DMA((tiles,)),
+        ],
+        compiler_params=pltpu.CompilerParams(
+            collective_id=0,
+            has_side_effects=True,
+            dimension_semantics=("arbitrary", "arbitrary"),
+            vmem_limit_bytes=60 * 1024 * 1024,
+        ),
+        name="bloch",
+    )(wq, wk, moved)
+    return result[..., :pairs]
+
+
+def sums_kernel(electron_ref, phonon_ref, electron_out, phonon_out, got_e, got_p, send, recv_e, recv_p):
+    bands, kas = lax.axis_size("pb"), lax.axis_size("ka")
+    my_pb, my_ka = lax.axis_index("pb"), lax.axis_index("ka")
+    barrier = pltpu.get_barrier_semaphore()
+    for step in range(1, bands):
+        pl.semaphore_signal(
+            barrier, inc=1, device_id={"pb": lax.rem(my_pb + step, bands), "ka": my_ka},
+            device_id_type=MESH,
+        )
+    for step in range(1, kas):
+        pl.semaphore_signal(
+            barrier, inc=1, device_id={"pb": my_pb, "ka": lax.rem(my_ka + step, kas)},
+            device_id_type=MESH,
+        )
+    pl.semaphore_wait(barrier, bands + kas - 2)
+    copies = []
+    for step in range(1, bands):
+        copies.append(pltpu.make_async_remote_copy(
+            electron_ref, got_e.at[my_pb], send.at[step - 1], recv_e.at[step - 1],
+            device_id={"pb": lax.rem(my_pb + step, bands), "ka": my_ka}, device_id_type=MESH,
+        ))
+    for step in range(1, kas):
+        copies.append(pltpu.make_async_remote_copy(
+            phonon_ref, got_p.at[my_ka], send.at[bands + step - 2], recv_p.at[step - 1],
+            device_id={"pb": my_pb, "ka": lax.rem(my_ka + step, kas)}, device_id_type=MESH,
+        ))
+    for copy in copies:
+        copy.start()
+    got_e[my_pb] = electron_ref[...]
+    got_p[my_ka] = phonon_ref[...]
+    for copy in copies:
+        copy.wait()
+    total = got_e[0]
+    for step in range(1, bands):
+        total = total + got_e[step]
+    electron_out[...] = total
+    total = got_p[0]
+    for step in range(1, kas):
+        total = total + got_p[step]
+    phonon_out[...] = total
+
+
+def exchange(electron, phonon):
+    bands, kas = lax.axis_size("pb"), lax.axis_size("ka")
+    whole = pl.BlockSpec(memory_space=pltpu.VMEM)
+    return pl.pallas_call(
+        sums_kernel,
+        in_specs=[whole, whole],
+        out_specs=[whole, whole],
+        out_shape=[
+            jax.ShapeDtypeStruct(electron.shape, electron.dtype),
+            jax.ShapeDtypeStruct(phonon.shape, phonon.dtype),
+        ],
+        scratch_shapes=[
+            pltpu.VMEM((bands, *electron.shape), jnp.float32),
+            pltpu.VMEM((kas, *phonon.shape), jnp.float32),
+            pltpu.SemaphoreType.DMA((bands + kas - 2,)),
+            pltpu.SemaphoreType.DMA((bands - 1,)),
+            pltpu.SemaphoreType.DMA((kas - 1,)),
+        ],
+        compiler_params=pltpu.CompilerParams(collective_id=1, has_side_effects=True),
+        name="sums",
+    )(electron, phonon)
 
 
 def on_device(
@@ -91,47 +316,26 @@
     k_local = energy_k.shape[0]
     q_local = frequencies.shape[0]
     cells_local = coupling.shape[1]
-    pairs_local = coupling.shape[2]
-    phonon_count = coupling.shape[3]
-    q_total = q_local * lax.axis_size("pb")
-    k_total = k_local * lax.axis_size("ka")
+    bands, kas = lax.axis_size("pb"), lax.axis_size("ka")
+    q_total = q_local * bands
+    k_total = k_local * kas
     cos_q, sin_q = phase_table(qpoints, phonon_cells)
-    cos_k, sin_k = phase_table(kpoints, electron_cells)
-    real_flat = coupling[0].reshape(cells_local * pairs_local, phonon_count)
-    imag_flat = coupling[1].reshape(cells_local * pairs_local, phonon_count)
-    half_real = (
-        (contract_last(cos_q, real_flat) - contract_last(sin_q, imag_flat))
-        .astype(jnp.bfloat16)
-        .reshape(q_total, cells_local, pairs_local)
-    )
-    half_imag = (
-        (contract_last(cos_q, imag_flat) + contract_last(sin_q, real_flat))
-        .astype(jnp.bfloat16)
-        .reshape(q_total, cells_local, pairs_local)
-    )
-    cell_start = lax.axis_index("ka") * cells_local
-    cos_cols = lax.dynamic_slice_in_dim(cos_k, cell_start, cells_local, 1)
-    sin_cols = lax.dynamic_slice_in_dim(sin_k, cell_start, cells_local, 1)
-    real_part = mixed("kr,qrp->kqp", cos_cols, half_real) - mixed(
-        "kr,qrp->kqp", sin_cols, half_imag
-    )
-    imag_part = mixed("kr,qrp->kqp", cos_cols, half_imag) + mixed(
-        "kr,qrp->kqp", sin_cols, half_real
-    )
-    partials = lax.psum_scatter(
-        jnp.stack([real_part, imag_part], axis=1), "ka", scatter_dimension=0, tiled=True
-    )
-    owned_real = partials[:, 0].astype(jnp.bfloat16)
-    owned_imag = partials[:, 1].astype(jnp.bfloat16)
-    bloch_real, bloch_imag = (
-        lax.all_to_all(owned_real, "pb", split_axis=1, concat_axis=2, tiled=True),
-        lax.all_to_all(owned_imag, "pb", split_axis=1, concat_axis=2, tiled=True),
-    )
-    bloch_real = bloch_real.reshape(k_local, q_local, NB, MODES)
-    bloch_imag = bloch_imag.reshape(k_local, q_local, NB, MODES)
+    own_cells = lax.dynamic_slice_in_dim(
+        electron_cells, lax.axis_index("ka") * cells_local, cells_local, 1
+    )
+    cos_k, sin_k = phase_table(kpoints, own_cells)
+    wq = jnp.concatenate(
+        [jnp.concatenate([cos_q, -sin_q], 1), jnp.concatenate([sin_q, cos_q], 1)], 0
+    )
+    wk = jnp.stack(
+        [jnp.concatenate([cos_k, -sin_k], 1), jnp.concatenate([sin_k, cos_k], 1)], 1
+    ).reshape(2 * k_total, 2 * cells_local)
+    values = bloch(coupling, wq, wk, q_local, k_local)
+    values = values.reshape(bands, q_local // 2, 2, k_local, 2, -1)
+    values = jnp.transpose(values, (4, 3, 1, 2, 0, 5)).reshape(2, k_local, q_local, NB, MODES)
     electron, phonon = widths(
-        bloch_real,
-        bloch_imag,
+        values[0],
+        values[1],
         phonon_modes,
         band_vectors,
         energies_kq,
@@ -141,8 +345,7 @@
         frequencies,
         bose_factors,
     )
-    electron_width = lax.psum(electron / (q_total * NB), "pb")
-    phonon_width = lax.psum(phonon / (k_total * NB), "ka")
+    electron_width, phonon_width = exchange(electron / (q_total * NB), phonon / (k_total * NB))
     return (electron_width, phonon_width)
 
 

time: 404 us -> 71.4 us (0.18)
  local copies, waits for them, and re-layouts: 228 us -> 9.68 us
  waiting for transfers between devices: 64.2 us -> 0 us
  matrix products: 63.3 us -> 2.06 us
  Pallas kernels: 0 us -> 53.6 us
  blocking collectives: 23.1 us -> 0 us
  between operations: 14.3 us -> 0.86 us
  starting transfers between devices: 7.27 us -> 0 us
    slice x3, local copies, waits for them, and re-layouts: 112 us -> 0.65 us  [the longest x2 0.56 us: on_device(): values[1]]
    another operation x3 -> x1, local copies, waits for them, and re-layouts: 95.7 us -> 0.02 us  [on_device(): jnp.stack([jnp.concatenate([cos_k, -sin_k], 1), jnp.concatenate([sin_k, c...]
    dot_general x4 -> x0, matrix products: 58.6 us -> none  [contract_last(): lax.dot_general(left, right, (((1,), (1,)), ((), ())), preferred_element_...]
    reduce_scatter x1 -> x0, waiting for transfers between devices: 54.3 us -> none  [on_device(): lax.psum_scatter(jnp.stack([real_part, imag_part], axis=1), 'ka', scatter...]
    pallas_call x0 -> x2, Pallas kernels: none -> 53.6 us  [the longest x1 46.7 us: bloch(): pl.pallas_call(functools.partial(bloch_kernel, cells_block, tile, last),...]
    psum x2 -> x0, blocking collectives: 23.1 us -> none  [the longest x1 12.4 us: on_device(): electron_width = lax.psum(electron / (q_total * NB), 'pb')]
    reshape x4 -> x2, local copies, waits for them, and re-layouts: 15.3 us -> 1.74 us  [the longest x1 1.11 us: on_device(): values = values.reshape(bands, q_local // 2, 2, k_local, 2, -1)]
    all_to_all x2 -> x0, waiting for transfers between devices: 9.82 us -> none  [the longest x1 5.09 us: on_device(): lax.all_to_all(owned_real, 'pb', split_axis=1, concat_axis=2, tiled=True)]
  transfers between devices with their start and end apart: 3 -> 0, of which waited for: 3 -> 0; matrix products, arithmetic and copies ran while one was open for 0% -> 0% of each run, Pallas kernels for 0% -> 0%
where the time goes in v1:
time: 71.4 us; the launch traced here: 70.7 us
  Pallas kernels  53.6 us (75%)
  local copies, waits for them, and re-layouts  9.68 us (14%)
  other arithmetic  4.48 us (6%)
  matrix products  2.06 us (3%)
  between operations  0.86 us (1%)
    pallas_call x1, Pallas kernels, bloch(): pl.pallas_call(functools.partial(bloch_kernel, cells_block, tile, last),...  46.7 us
    pallas_call x1, Pallas kernels, exchange(): pl.pallas_call(sums_kernel, in_specs=[whole, whole], out_specs=[whole, wh...  6.86 us
    unnamed x14, local copies, waits for them, and re-layouts  3.42 us
    dot_general x8, matrix products, mixed(): return jnp.einsum(form, left, right, preferred_element_type=jnp.float32)  2.06 us
    mul x3, local copies, waits for them, and re-layouts, phase_table(): points[0][:, None] * cells[0][None, :]  1.6 us

profile of v1, /device:TPU:0, one launch (start us, length us, event | category | flops | bytes accessed | tf_op | source)
XLA Modules:
  0.0 70.7 jit_solution(11775187349372291795)
XLA Ops:
  0.6 0.0 copy-start
  0.6 0.0 copy-start.1
  0.7 0.0 copy-start.3
  0.7 0.0 copy-start.4
  0.7 0.0 copy-start.2
  0.7 0.6 copy-done
  1.3 0.1 constant_dynamic-slice_fusion
  1.4 0.8 %slice_bitcast_fusion.5 = (s32[16]{0:T(128)S(1)}, s32[16]{0:T(128)S(1)}, s32[16]{0:T(128)S(1)}) fusion(s32[3,16]{1,0:T(4,128)} %param.14), kind=kLoop, calls=%fused_computation.70 | loop fusion | bytes 384 | tf_op jit(solution)/shard_map/mul | solution.py:21
  2.2 0.8 %slice_bitcast_fusion.8 = (s32[32]{0:T(128)S(1)}, s32[32]{0:T(128)S(1)}, s32[32]{0:T(128)S(1)}) fusion(s32[3,32]{1,0:T(4,128)} %param.15), kind=kLoop, calls=%fused_computation.73 | loop fusion | bytes 768 | tf_op jit(solution)/shard_map/mul | solution.py:21
  3.0 0.7 broadcast_add_fusion
  3.7 0.1 fusion.38
  3.8 0.1 sine_convert_fusion.1
  4.0 0.1 maximum_bitcast_fusion
  4.1 0.6 reshape.36.wk_ref
  4.7 0.8 %slice_reduce_fusion.2 = (s32[320]{0:T(512)S(1)}, s32[320]{0:T(512)S(1)}, s32[320]{0:T(512)S(1)}) fusion(s32[3,320]{1,0:T(4,128)} %param.17), kind=kLoop, calls=%fused_computation.61 | loop fusion | bytes 7680 | tf_op jit(solution)/shard_map/slice | solution.py:21
  5.5 0.8 %subtract_bitcast_fusion = f32[4,4,40]{2,0,1:T(4,128)S(1)} fusion(f32[4,4,40]{2,1,0:T(4,128)} %param.20, f32[4]{0:T(128)} %param.22), kind=kLoop, calls=%fused_computation.51 | loop fusion | flops 640 | bytes 5136 | tf_op jit(solution)/shard_map/sub | solution.py:67
  6.3 0.8 %broadcast_subtract_fusion = f32[4,4,40]{2,0,1:T(4,128)S(1)} fusion(f32[4]{0:T(128)} %param.23, f32[4,4,40]{2,1,0:T(4,128)} %param.21), kind=kLoop, calls=%fused_computation.58 | loop fusion | flops 640 | bytes 5136 | tf_op jit(solution)/shard_map/sub | solution.py:75
  7.1 0.7 copy.40
  7.8 0.3 fusion.39
  8.1 0.3 sine_convert_fusion
  8.4 0.7 %maximum_maximum_fusion.wq_ref = bf16[64,640]{1,0:T(8,128)(2,1)} fusion(bf16[32,320]{1,0:T(8,128)(2,1)S(1)} %get-tuple-element.12, bf16[32,320]{1,0:T(8,128)(2,1)S(1)} %get-tuple-element.11, bf16[32,320]{1,0:T(8,128)(2,1)S(1)} %fusion.39), kind=kLoop, calls=%fused_computation.35 | loop fusion | flops 327680 | bytes 143360 | tf_op jit(solution)/shard_map/concatenate | solution.py:327
  9.1 46.7 %bloch.1 = bf16[8,2,16,640]{3,2,1,0:T(8,128)(2,1)} custom-call(bf16[64,640]{1,0:T(8,128)(2,1)} %maximum_maximum_fusion.wq_ref, bf16[32,160]{1,0:T(8,128)(2,1)} %reshape.36.wk_ref, bf16[2,80,320,600]{3,2,1,0:T(8,128)(2,1)} %bitcast.81), custom_call_target="tpu_custom_call" | custom-call | tf_op jit(solution)/shard_map/bloch/pallas_call | solution.py:208
  55.9 1.1 %reshape.37 = bf16[8,2,2,4,2,600]{5,4,3,2,1,0:T(2,128)(2,1)S(1)} reshape(bf16[8,2,16,600]{3,2,1,0:T(8,128)(2,1)} %bitcast.83) | data formatting | bytes 614400 | tf_op jit(solution)/shard_map/reshape | solution.py:334
  57.0 0.5 fusion.41
  57.4 0.1 copy.32
  57.5 0.3 squeeze.20
  57.9 0.1 copy.30
  58.0 0.3 squeeze.18
  58.3 0.0 copy-done.1
  58.3 0.2 fusion.18
  58.5 0.2 fusion.6
  58.8 0.2 fusion.22
  59.0 0.2 fusion.7
  59.2 0.0 copy-done.2
  59.3 0.1 copy.48
  59.4 0.1 copy.47
  59.6 0.2 fusion.10
  59.8 0.2 fusion.12
  60.0 0.2 fusion.3
  60.3 0.0 copy-done.3
  60.3 0.0 copy-done.4
  60.3 0.5 multiply_reduce_fusion
  60.7 0.6 broadcast_multiply_fusion
  61.3 6.9 %sums.1 = (f32[4,120]{1,0:T(4,128)}, f32[4,120]{1,0:T(4,128)}) custom-call(f32[4,120]{1,0:T(4,128)} %get-tuple-element.27.electron_ref, f32[4,120]{1,0:T(4,128)} %get-tuple-element.26.phonon_ref), custom_call_target="tpu_custom_call" | custom-call | tf_op jit(solution)/shard_map/sums/pallas_call | solution.py:281
  68.2 1.2 %copy.61 = f32[4,120]{1,0:T(4,128)} copy(f32[4,120]{1,0:T(4,128)} %get-tuple-element.30) | data formatting | bytes 3840
  69.5 1.2 %copy.62 = f32[4,120]{1,0:T(4,128)} copy(f32[4,120]{1,0:T(4,128)} %get-tuple-element.31) | data formatting | bytes 3840
  (6 shorter events, 0.1 us)
Async XLA Ops:
  0.6 0.7 copy-start
  0.6 57.6 %copy-start.1 = (bf16[4,2,120,120]{3,2,1,0:T(8,128)(2,1)S(1)}, bf16[4,2,120,120]{3,2,1,0:T(8,128)(2,1)}, u32[]{:S(2)}) copy-start(bf16[4,2,120,120]{3,2,1,0:T(8,128)(2,1)} %param.18) | copy-start | bytes 691204
  0.7 59.6 %copy-start.3 = (f32[4,120]{1,0:T(4,128)S(1)}, f32[4,120]{1,0:T(4,128)}, u32[]{:S(2)}) copy-start(f32[4,120]{1,0:T(4,128)} %param.25) | copy-start | bytes 5764
  0.7 59.6 %copy-start.4 = (f32[4,120]{1,0:T(4,128)S(1)}, f32[4,120]{1,0:T(4,128)}, u32[]{:S(2)}) copy-start(f32[4,120]{1,0:T(4,128)} %param.24) | copy-start | bytes 5764
  0.7 58.6 %copy-start.2 = (bf16[4,4,2,40,40]{4,3,2,1,0:T(8,128)(2,1)S(1)}, bf16[4,4,2,40,40]{4,3,2,1,0:T(8,128)(2,1)}, u32[]{:S(2)}) copy-start(bf16[4,4,2,40,40]{4,3,2,1,0:T(8,128)(2,1)} %param.19) | copy-start | bytes 307204

commit v2 on v1

--- a/solution.py
+++ b/solution.py
@@ -298,6 +298,307 @@
     )(electron, phonon)
 
 
+def angles(points, cells):
+    product = lax.dot_general(
+        points.astype(jnp.float32).astype(jnp.bfloat16),
+        cells.astype(jnp.float32).astype(jnp.bfloat16),
+        (((0,), (0,)), ((), ())),
+        preferred_element_type=jnp.float32,
+    )
+    turns = jnp.floor((product + 0.5) * (1.0 / NG))
+    angle = (product - turns * NG) * (2.0 * math.pi / NG)
+    return jnp.cos(angle), jnp.sin(angle)
+
+
+def whole_kernel(
+    cells_block, tile, last, kpoints, qpoints, electron_cells, phonon_cells, modes, vectors,
+    levels, filled, energy_k, occupation_k, omega, bose, x_ref, out_ref,
+    wq, wk, half, parts, recv, rows_ref, emission, absorption, totals, got_e, got_p,
+    send_sem, recv_sem, send_e, recv_e, send_p, recv_p,
+):
+    pairs_step = pl.program_id(0)
+    cell_step = pl.program_id(1)
+    tiles = pl.num_programs(0)
+    cell_steps = pl.num_programs(1)
+    bands, kas = lax.axis_size("pb"), lax.axis_size("ka")
+    devices = bands * kas
+    my_pb, my_ka = lax.axis_index("pb"), lax.axis_index("ka")
+    me = my_pb * kas + my_ka
+    columns = wq.shape[0]
+    q_total = columns // 2
+    cells = half.shape[1] // columns
+    groups = parts.shape[2]
+    mine = groups // bands
+    rows = parts.shape[3] // 2
+    q_local, k_local = vectors.shape[0], vectors.shape[1]
+    barrier = pltpu.get_barrier_semaphore()
+
+    @pl.when((pairs_step == 0) & (cell_step == 0))
+    def _():
+        def greet(step, carry):
+            peer = lax.rem(me + step, devices)
+            pl.semaphore_signal(
+                barrier, inc=1, device_id={"pb": peer // kas, "ka": lax.rem(peer, kas)},
+                device_id_type=MESH,
+            )
+            return carry
+
+        lax.fori_loop(1, devices, greet, 0)
+        cos, sin = angles(qpoints[...], phonon_cells[...])
+        wq[...] = jnp.concatenate(
+            [jnp.concatenate([cos, -sin], 1), jnp.concatenate([sin, cos], 1)], 0
+        ).astype(jnp.bfloat16)
+        table = electron_cells[...]
+        own = table[:, :cells]
+        for ka in range(1, kas):
+            own = jnp.where(my_ka == ka, table[:, ka * cells : (ka + 1) * cells], own)
+        cos, sin = angles(kpoints[...], own)
+        blocks = []
+        for ka in range(kas):
+            c = cos[ka * k_local : (ka + 1) * k_local]
+            s = sin[ka * k_local : (ka + 1) * k_local]
+            blocks += [jnp.concatenate([c, -s], 1), jnp.concatenate([s, c], 1)]
+        wk[...] = jnp.concatenate(blocks, 0).astype(jnp.bfloat16)
+
+    @pl.when((pairs_step == 0) & (cell_step == 1))
+    def _():
+        for q in range(q_local):
+            freq = omega[q : q + 1, :]
+            boson = bose[q : q + 1, :]
+            level_q = jnp.transpose(levels[q])
+            filled_q = jnp.transpose(filled[q])
+            for k in range(k_local):
+                f = filled_q[:, k : k + 1]
+                offset = energy_k[k] - level_q[:, k : k + 1]
+                absorb = gaussian(offset + freq)
+                emit = gaussian(offset - freq)
+                emission[q, k] = (boson + f) * absorb + (boson + 1.0 - f) * emit
+                absorption[q, k] = (occupation_k[k] - f) * absorb
+
+    for cell in range(cells_block):
+        right = jnp.concatenate([x_ref[0, cell], x_ref[1, cell]], axis=0)
+        product = jnp.dot(wq[...], right, preferred_element_type=jnp.float32)
+        row = cell_step * cells_block + cell
+        for lane in range(tile // LANES):
+            half[lane, pl.ds(row, columns, stride=cells), :] = product[
+                :, lane * LANES : (lane + 1) * LANES
+            ]
+
+    def strip(index):
+        start = pl.multiple_of(index * cells, cells)
+        return jnp.concatenate(
+            [half[lane, pl.ds(start, cells), :] for lane in range(tile // LANES)], axis=1
+        ).astype(jnp.bfloat16)
+
+    @pl.when(cell_step == cell_steps - 1)
+    def _():
+        def contract(group, carry):
+            sums = []
+            for member in range(2):
+                q = group * 2 + member
+                right = jnp.concatenate([strip(q), strip(q_total + q)], axis=0)
+                sums.append(jnp.dot(wk[...], right, preferred_element_type=jnp.float32))
+            for ka in range(kas):
+                block = slice(ka * rows, (ka + 1) * rows)
+                parts[pairs_step, ka, group] = jnp.concatenate(
+                    [sums[0][block], sums[1][block]], axis=0
+                ).astype(jnp.bfloat16)
+            return carry
+
+        lax.fori_loop(0, groups, contract, 0, unroll=4)
+
+    @pl.when((cell_step == cell_steps - 1) & (pairs_step == 0))
+    def _():
+        pl.semaphore_wait(barrier, devices - 1)
+
+    def send(index, width):
+        def one(step, carry):
+            peer = lax.rem(me + step, devices)
+            to_pb, to_ka = peer // kas, lax.rem(peer, kas)
+            pltpu.make_async_remote_copy(
+                src_ref=parts.at[index, to_ka, pl.ds(to_pb * mine, mine), :, pl.ds(0, width)],
+                dst_ref=recv.at[index, me, :, :, pl.ds(0, width)],
+                send_sem=send_sem.at[index],
+                recv_sem=recv_sem.at[index],
+                device_id={"pb": to_pb, "ka": to_ka},
+                device_id_type=MESH,
+            ).start()
+            return carry
+
+        lax.fori_loop(1, devices, one, 0)
+
+    @pl.when((cell_step == cell_steps - 1) & (pairs_step < tiles - 1))
+    def _():
+        send(pairs_step, tile)
+
+    @pl.when((cell_step == cell_steps - 1) & (pairs_step == tiles - 1))
+    def _():
+        count = recv.shape[0]
+        send(count - 1, last)
+        for index in range(count):
+            recv[index, me] = parts[index, my_ka, pl.ds(my_pb * mine, mine)]
+        bands_n = rows_ref.shape[0] // (mine * 2 * rows)
+        bands_own = bands_n // bands
+
+        def piece(band, group, start):
+            stop = start + MODES
+            first, final = start // tile, (stop - 1) // tile
+            out = []
+            for index in range(first, final + 1):
+                low, high = max(start, index * tile), min(stop, (index + 1) * tile)
+                aligned = (low - index * tile) // LANES * LANES
+                upper = -(-(high - index * tile) // LANES) * LANES
+                total = recv[index, band * kas, group, :, aligned:upper].astype(jnp.float32)
+                for ka in range(1, kas):
+                    total = total + recv[
+                        index, band * kas + ka, group, :, aligned:upper
+                    ].astype(jnp.float32)
+                out.append(
+                    total[:, low - index * tile - aligned : high - index * tile - aligned]
+                )
+            return out[0] if len(out) == 1 else jnp.concatenate(out, axis=1)
+
+        for index in range(count):
+            width = tile if index < count - 1 else last
+            window = recv.at[index, pl.ds(1, devices - 1), :, :, pl.ds(0, width)]
+            pltpu.make_async_copy(window, window, recv_sem.at[index]).wait()
+            for n in range(bands_own):
+                if (n * MODES + MODES - 1) // tile != index:
+                    continue
+                for band in range(bands):
+                    for group in range(mine):
+                        row = group * 2 * rows * bands_n + band * bands_own + n
+                        rows_ref[pl.ds(row, 2 * rows, stride=bands_n), :MODES] = piece(
+                            band, group, n * MODES
+                        )
+        per_q = rows * bands_n
+        side = per_q // 2
+        electron = [None] * k_local
+        for q in range(q_local):
+            left = rows_ref[q * per_q : (q + 1) * per_q, :MODES].astype(jnp.bfloat16)
+            by_real = jnp.dot(left, modes[q, 0], preferred_element_type=jnp.float32)
+            by_imag = jnp.dot(left, modes[q, 1], preferred_element_type=jnp.float32)
+            moded_real = by_real[:side] - by_imag[side:]
+            moded_imag = by_imag[:side] + by_real[side:]
+            phonon = None
+            for k in range(k_local):
+                u = jnp.concatenate(
+                    [vectors[q, k, 0].astype(jnp.float32), vectors[q, k, 1].astype(jnp.float32)], 0
+                ).astype(jnp.bfloat16)
+                real = moded_real[k * bands_n : (k + 1) * bands_n]
+                imag = moded_imag[k * bands_n : (k + 1) * bands_n]
+                over = (((0,), (0,)), ((), ()))
+                band_real = lax.dot_general(
+                    u, jnp.concatenate([real, imag], 0).astype(jnp.bfloat16), over,
+                    preferred_element_type=jnp.float32,
+                )
+                band_imag = lax.dot_general(
+                    u, jnp.concatenate([imag, -real], 0).astype(jnp.bfloat16), over,
+                    preferred_element_type=jnp.float32,
+                )
+                weight = band_real * band_real + band_imag * band_imag
+                e_term = weight * emission[q, k]
+                p_term = weight * absorption[q, k]
+                electron[k] = e_term if q == 0 else electron[k] + e_term
+                phonon = p_term if k == 0 else phonon + p_term
+            totals[1, q : q + 1, :] = jnp.sum(phonon, axis=0, keepdims=True)
+        for k in range(k_local):
+            totals[0, k : k + 1, :] = jnp.sum(electron[k], axis=0, keepdims=True)
+        copies = []
+        for step in range(1, bands):
+            copies.append(pltpu.make_async_remote_copy(
+                totals.at[0], got_e.at[my_pb], send_e.at[step - 1], recv_e.at[step - 1],
+                device_id={"pb": lax.rem(my_pb + step, bands), "ka": my_ka}, device_id_type=MESH,
+            ))
+        for step in range(1, kas):
+            copies.append(pltpu.make_async_remote_copy(
+                totals.at[1], got_p.at[my_ka], send_p.at[step - 1], recv_p.at[step - 1],
+                device_id={"pb": my_pb, "ka": lax.rem(my_ka + step, kas)}, device_id_type=MESH,
+            ))
+        for copy in copies:
+            copy.start()
+        got_e[my_pb] = totals[0]
+        got_p[my_ka] = totals[1]
+        for index in range(count):
+            width = tile if index < count - 1 else last
+            window = recv.at[index, pl.ds(1, devices - 1), :, :, pl.ds(0, width)]
+            pltpu.make_async_copy(window, window, send_sem.at[index]).wait()
+        for copy in copies:
+            copy.wait()
+        total = got_e[0]
+        for step in range(1, bands):
+            total = total + got_e[step]
+        out_ref[0] = total
+        total = got_p[0]
+        for step in range(1, kas):
+            total = total + got_p[step]
+        out_ref[1] = total
+
+
+def everything(
+    coupling, kpoints, qpoints, electron_cells, phonon_cells, phonon_modes, band_vectors,
+    energies_kq, occupations_kq, energy_k, occupation_k, frequencies, bose_factors,
+):
+    bands, kas = lax.axis_size("pb"), lax.axis_size("ka")
+    devices = bands * kas
+    parts_count, cells, pairs, phonons = coupling.shape
+    moved = jnp.transpose(coupling, (0, 1, 3, 2))
+    padded = -(-pairs // LANES) * LANES
+    tile = min(2 * LANES, padded)
+    tiles = -(-padded // tile)
+    last = padded - (tiles - 1) * tile
+    cells_block = 16
+    q_local, k_local = band_vectors.shape[0], band_vectors.shape[1]
+    bands_n = band_vectors.shape[3]
+    columns = 2 * qpoints.shape[1]
+    groups = columns // 4
+    mine = q_local // 2
+    rows = 2 * k_local
+    small = pl.BlockSpec(memory_space=pltpu.VMEM)
+    scalars = pl.BlockSpec(memory_space=pltpu.SMEM)
+    dma = pltpu.SemaphoreType.DMA
+    result = pl.pallas_call(
+        functools.partial(whole_kernel, cells_block, tile, last),
+        grid=(tiles, cells // cells_block),
+        in_specs=[small] * 8
+        + [scalars] * 2
+        + [small] * 2
+        + [pl.BlockSpec((parts_count, cells_block, phonons, tile), lambda t, e: (0, e, 0, t))],
+        out_specs=small,
+        out_shape=jax.ShapeDtypeStruct((2, k_local, MODES), jnp.float32),
+        scratch_shapes=[
+            pltpu.VMEM((columns, 2 * phonons), jnp.bfloat16),
+            pltpu.VMEM((2 * k_local * kas, 2 * cells), jnp.bfloat16),
+            pltpu.VMEM((tile // LANES, columns * cells, LANES), jnp.float32),
+            pltpu.VMEM((tiles, kas, groups, 2 * rows, tile), jnp.bfloat16),
+            pltpu.VMEM((tiles, devices, mine, 2 * rows, tile), jnp.bfloat16),
+            pltpu.VMEM((q_local * rows * bands_n, LANES), jnp.float32),
+            pltpu.VMEM((q_local, k_local, bands_n, MODES), jnp.float32),
+            pltpu.VMEM((q_local, k_local, bands_n, MODES), jnp.float32),
+            pltpu.VMEM((2, k_local, MODES), jnp.float32),
+            pltpu.VMEM((bands, k_local, MODES), jnp.float32),
+            pltpu.VMEM((kas, k_local, MODES), jnp.float32),
+            dma((tiles,)),
+            dma((tiles,)),
+            dma((bands - 1,)),
+            dma((bands - 1,)),
+            dma((kas - 1,)),
+            dma((kas - 1,)),
+        ],
+        compiler_params=pltpu.CompilerParams(
+            collective_id=2,
+            has_side_effects=True,
+            dimension_semantics=("arbitrary", "arbitrary"),
+            vmem_limit_bytes=60 * 1024 * 1024,
+        ),
+        name="widths",
+    )(
+        kpoints, qpoints, electron_cells, phonon_cells, phonon_modes, band_vectors, energies_kq,
+        occupations_kq, energy_k, occupation_k, frequencies, bose_factors, moved,
+    )
+    return result
+
+
 def on_device(
     coupling,
     kpoints,
@@ -319,6 +620,12 @@
     bands, kas = lax.axis_size("pb"), lax.axis_size("ka")
     q_total = q_local * bands
     k_total = k_local * kas
+    if coupling.shape[2] % MODES == 0 and k_local == q_local:
+        sums = everything(
+            coupling, kpoints, qpoints, electron_cells, phonon_cells, phonon_modes, band_vectors,
+            energies_kq, occupations_kq, energy_k, occupation_k, frequencies, bose_factors,
+        )
+        return (sums[0] / (q_total * NB), sums[1] / (k_total * NB))
     cos_q, sin_q = phase_table(qpoints, phonon_cells)
     own_cells = lax.dynamic_slice_in_dim(
         electron_cells, lax.axis_index("ka") * cells_local, cells_local, 1

time: 71.4 us -> 54.8 us (0.77)
  local copies, waits for them, and re-layouts: 9.68 us -> 0 us
  other arithmetic: 4.48 us -> 1.26 us
  matrix products: 2.06 us -> 0 us
  Pallas kernels: 53.6 us -> 52.5 us
    unnamed x14 -> x0, local copies, waits for them, and re-layouts: 3.42 us -> none
    dot_general x8 -> x0, matrix products: 2.06 us -> none  [mixed(): return jnp.einsum(form, left, right, preferred_element_type=jnp.float32)]
    reshape x2 -> x0, local copies, waits for them, and re-layouts: 1.74 us -> none  [the longest x1 1.11 us: on_device(): values = values.reshape(bands, q_local // 2, 2, k_local, 2, -1)]
    mul x3 -> x0, local copies, waits for them, and re-layouts: 1.6 us -> none  [phase_table(): points[0][:, None] * cells[0][None, :]]
    sub x2 -> x0, other arithmetic: 1.56 us -> none  [the longest x1 0.79 us: widths(): occupation_k[:, None, None, None] - filled_kq]
    slice x5 -> x0, local copies, waits for them, and re-layouts: 1.51 us -> none  [the longest x1 0.83 us: phase_table(): cells[0][None, :]]
    pallas_call x2 -> x1, Pallas kernels: 53.6 us -> 52.5 us  [everything(): pl.pallas_call(functools.partial(whole_kernel, cells_block, tile, last),...]
where the time goes in v2:
time: 54.8 us; the launch traced here: 54.4 us
  Pallas kernels  52.5 us (96%)
  other arithmetic  1.26 us (2%)
  between operations  0.64 us (1%)
    pallas_call x1, Pallas kernels, everything(): pl.pallas_call(functools.partial(whole_kernel, cells_block, tile, last),...  52.5 us
    div x1, other arithmetic, on_device(): return (sums[0] / (q_total * NB), sums[1] / (k_total * NB))  1.26 us

profile of v2, /device:TPU:0, one launch (start us, length us, event | category | flops | bytes accessed | tf_op | source)
XLA Modules:
  0.0 54.4 jit_solution(10682662082296736539)
XLA Ops:
  0.6 52.5 %widths.1 = f32[2,4,120]{2,1,0:T(4,128)} custom-call(s32[3,16]{1,0:T(4,128)} %kpoints.1, s32[3,32]{1,0:T(4,128)} %qpoints.1, s32[3,320]{1,0:T(4,128)} %electron_cells.1, s32[3,320]{1,0:T(4,128)} %phonon_cells.1, bf16[4,2,120,120]{3,2,1,0:T(8,128)(2,1)} %modes.1, bf16[4,4,2,40,40]{4,3,2,1,0:T(8,128)(2,1)} %vectors.1, f32[4,4,40]{2,1,0:T(4,128)} %levels.1, ...), custom_call_target="tpu_custom_call" | custom-call | tf_op jit(solution)/shard_map/widths/pallas_call | solution.py:560
  53.2 1.3 %multiply_bitcast_fusion = (f32[4,120]{1,0:T(4,128)}, f32[4,120]{1,0:T(4,128)}) fusion(f32[2,4,120]{2,1,0:T(4,128)} %widths.1), kind=kLoop, calls=%fused_computation | loop fusion | flops 960 | bytes 7680 | tf_op jit(solution)/shard_map/div | solution.py:628

commit v3 on v2

--- a/solution.py
+++ b/solution.py
@@ -360,7 +360,7 @@
             blocks += [jnp.concatenate([c, -s], 1), jnp.concatenate([s, c], 1)]
         wk[...] = jnp.concatenate(blocks, 0).astype(jnp.bfloat16)
 
-    @pl.when((pairs_step == 0) & (cell_step == 1))
+    @pl.when((pairs_step == jnp.minimum(tiles - 1, 1)) & (cell_step == 0))
     def _():
         for q in range(q_local):
             freq = omega[q : q + 1, :]
@@ -375,14 +375,19 @@
                 emission[q, k] = (boson + f) * absorb + (boson + 1.0 - f) * emit
                 absorption[q, k] = (occupation_k[k] - f) * absorb
 
-    for cell in range(cells_block):
-        right = jnp.concatenate([x_ref[0, cell], x_ref[1, cell]], axis=0)
-        product = jnp.dot(wq[...], right, preferred_element_type=jnp.float32)
-        row = cell_step * cells_block + cell
-        for lane in range(tile // LANES):
-            half[lane, pl.ds(row, columns, stride=cells), :] = product[
-                :, lane * LANES : (lane + 1) * LANES
-            ]
+    def project(chunk, carry):
+        for step in range(cells_block // 2):
+            cell = chunk * (cells_block // 2) + step
+            right = jnp.concatenate([x_ref[0, cell], x_ref[1, cell]], axis=0)
+            product = jnp.dot(wq[...], right, preferred_element_type=jnp.float32)
+            row = cell_step * cells_block + cell
+            for lane in range(tile // LANES):
+                half[lane, pl.ds(row, columns, stride=cells), :] = product[
+                    :, lane * LANES : (lane + 1) * LANES
+                ]
+        return carry
+
+    lax.fori_loop(0, 2, project, 0)
 
     def strip(index):
         start = pl.multiple_of(index * cells, cells)
@@ -544,10 +549,10 @@
     parts_count, cells, pairs, phonons = coupling.shape
     moved = jnp.transpose(coupling, (0, 1, 3, 2))
     padded = -(-pairs // LANES) * LANES
-    tile = min(2 * LANES, padded)
+    tile = LANES
     tiles = -(-padded // tile)
     last = padded - (tiles - 1) * tile
-    cells_block = 16
+    cells_block = cells
     q_local, k_local = band_vectors.shape[0], band_vectors.shape[1]
     bands_n = band_vectors.shape[3]
     columns = 2 * qpoints.shape[1]

time: 54.8 us -> 50.9 us (0.929)
  Pallas kernels: 52.5 us -> 48.8 us
    pallas_call x1, Pallas kernels: 52.5 us -> 48.8 us  [everything(): pl.pallas_call(functools.partial(whole_kernel, cells_block, tile, last),...]
where the time goes in v3:
time: 50.9 us; the launch traced here: 50.7 us
  Pallas kernels  48.8 us (96%)
  other arithmetic  1.26 us (2%)
  between operations  0.64 us (1%)
    pallas_call x1, Pallas kernels, everything(): pl.pallas_call(functools.partial(whole_kernel, cells_block, tile, last),...  48.8 us
    div x1, other arithmetic, on_device(): return (sums[0] / (q_total * NB), sums[1] / (k_total * NB))  1.26 us

profile of v3, /device:TPU:0, one launch (start us, length us, event | category | flops | bytes accessed | tf_op | source)
XLA Modules:
  0.0 50.7 jit_solution(73883750027244510)
XLA Ops:
  0.6 48.8 %widths.1 = f32[2,4,120]{2,1,0:T(4,128)} custom-call(s32[3,16]{1,0:T(4,128)} %kpoints.1, s32[3,32]{1,0:T(4,128)} %qpoints.1, s32[3,320]{1,0:T(4,128)} %electron_cells.1, s32[3,320]{1,0:T(4,128)} %phonon_cells.1, bf16[4,2,120,120]{3,2,1,0:T(8,128)(2,1)} %modes.1, bf16[4,4,2,40,40]{4,3,2,1,0:T(8,128)(2,1)} %vectors.1, f32[4,4,40]{2,1,0:T(4,128)} %levels.1, ...), custom_call_target="tpu_custom_call" | custom-call | tf_op jit(solution)/shard_map/widths/pallas_call | solution.py:565
  49.4 1.3 %multiply_bitcast_fusion = (f32[4,120]{1,0:T(4,128)}, f32[4,120]{1,0:T(4,128)}) fusion(f32[2,4,120]{2,1,0:T(4,128)} %widths.1), kind=kLoop, calls=%fused_computation | loop fusion | flops 960 | bytes 7680 | tf_op jit(solution)/shard_map/div | solution.py:633
